TPU v7x, 32 devices: a whole 2x2x4 slice. The times are simulated.
32 devices in a mesh: px: 8 (over z, core), py: 4 (over y, x).
Axes of the slice: x: 2, y: 2, z: 4, core: 2. Of those that a mesh axis runs over, the one named last changes fastest.
Arguments:
- initial_heat_state: float32 [4, 1024, 1024], P(None, 'px', 'py'), may hold values from -6 to 7
- spreading_coefficient: float32 [4, 1024, 1024], P(None, 'px', 'py'), may hold values from 0.5 to 200000, as said below
Outputs:
- heat: float32 [4, 1024, 1024], P(None, 'px', 'py')
Inputs may be any that keep to these rules, and one draw needn't show every extreme that they name: `spreading_coefficient`: positive in every cell.
All inputs are finite; a program needn't handle non-finite values.
Results may differ from a plain program's by a relative error of at most 0.0004.
Values sent between devices are 32-bit elements; how exact they have to be, the bound alone decides.
A program may use at most 64 MiB of HBM per device.

v0:
```python
import jax
import jax.numpy as jnp
from jax import lax
from jax.sharding import PartitionSpec as P


def with_halo(block, sides, width):
    for axis, dim in sides:
        count = lax.axis_size(axis)
        forward = [(i, i + 1) for i in range(count - 1)]
        backward = [(target, source) for source, target in forward]
        low = lax.ppermute(
            lax.slice_in_dim(block, block.shape[dim] - width, None, axis=dim), axis, forward
        )
        high = lax.ppermute(lax.slice_in_dim(block, 0, width, axis=dim), axis, backward)
        block = jnp.concatenate([low, block, high], axis=dim)
    return block


def partition(lower, middle, upper, source):
    length = lower.shape[1]
    ratios = []
    value_field = []
    left_resp = []
    right_resp = []
    for position in range(1, length - 1):
        low_now = lower[:, position]
        mid_now = middle[:, position]
        up_now = upper[:, position]
        src_now = source[:, position]
        if position == 1:
            divisor = mid_now
            value_num = src_now
            left_num = -low_now
            forcing_vector = jnp.zeros_like(src_now)
        else:
            divisor = mid_now - low_now * ratios[-1]
            value_num = src_now - low_now * value_field[-1]
            left_num = -low_now * left_resp[-1]
            forcing_vector = -low_now * right_resp[-1]
        if position == length - 2:
            forcing_vector = forcing_vector - up_now
        ratios.append(up_now / divisor)
        value_field.append(value_num / divisor)
        left_resp.append(left_num / divisor)
        right_resp.append(forcing_vector / divisor)
    for back_pos in range(length - 4, -1, -1):
        value_field[back_pos] = value_field[back_pos] - ratios[back_pos] * value_field[back_pos + 1]
        left_resp[back_pos] = left_resp[back_pos] - ratios[back_pos] * left_resp[back_pos + 1]
        right_resp[back_pos] = right_resp[back_pos] - ratios[back_pos] * right_resp[back_pos + 1]
    first_rows = (
        lower[:, 0],
        middle[:, 0] + upper[:, 0] * left_resp[0],
        upper[:, 0] * right_resp[0],
        source[:, 0] - upper[:, 0] * value_field[0],
    )
    last_rows = (
        lower[:, -1] * left_resp[-1],
        middle[:, -1] + lower[:, -1] * right_resp[-1],
        upper[:, -1],
        source[:, -1] - lower[:, -1] * value_field[-1],
    )
    return (
        jnp.stack(value_field, axis=1),
        jnp.stack(left_resp, axis=1),
        jnp.stack(right_resp, axis=1),
        first_rows + last_rows,
    )


def reduced_solve(rows):
    parts = rows.shape[1]
    width = rows.shape[2]

    def woven(first, last):
        return jnp.stack([first, last], axis=1).reshape(2 * parts, width)

    lower = woven(rows[0], rows[4])
    middle = woven(rows[1], rows[5])
    upper = woven(rows[2], rows[6])
    source = woven(rows[3], rows[7])
    zero = jnp.zeros((width,), jnp.float32)

    def forward(carry, inputs):
        ratio, value = carry
        low_now, mid_now, up_now, src_now = inputs
        divisor = mid_now - low_now * ratio
        ratio_new = up_now / divisor
        value_new = (src_now - low_now * value) / divisor
        return ((ratio_new, value_new), (ratio_new, value_new))

    carried, (ratios, value_field) = lax.scan(
        forward, (zero, zero), (lower, middle, upper, source), unroll=16
    )

    def backward(later, inputs):
        ratio, value = inputs
        now = value - ratio * later
        return (now, now)

    carried, solved = lax.scan(backward, zero, (ratios, value_field), reverse=True, unroll=16)
    return solved.reshape(parts, 2, width).transpose(1, 0, 2)


def interface_x(rows):
    plane_shape = rows[0].shape
    piled_arrays = jnp.stack(rows).reshape(8, -1)
    whole = lax.all_gather(piled_arrays[:, None], "px", axis=1, tiled=True)
    ends = lax.dynamic_slice_in_dim(reduced_solve(whole), lax.axis_index("px"), 1, 1)[:, 0]
    return (ends[0].reshape(plane_shape), ends[1].reshape(plane_shape))


def boundary_rows_column(rows):
    plane_shape = rows[0].shape
    piled_arrays = jnp.stack(rows).reshape(8, -1)
    whole = lax.all_gather(piled_arrays[:, None], "py", axis=1, tiled=True)
    ends = lax.dynamic_slice_in_dim(reduced_solve(whole), lax.axis_index("py"), 1, 1)[:, 0]
    return (ends[0].reshape(plane_shape), ends[1].reshape(plane_shape))


def banded_linear_sweep(spreading_coefficient, source, boundary_rows):
    length = source.shape[0]
    shape_rest = source.shape[1:]
    block = 16
    count = length // block

    def tiled_grid(array):
        return array.reshape((count, block) + shape_rest)

    def paired(first, last):
        return jnp.stack([first, last], axis=1).reshape((1, 2 * count) + shape_rest)

    lower = -spreading_coefficient
    middle = 1.0 + 2.0 * spreading_coefficient
    value_field, left_resp, right_resp, rows = partition(
        tiled_grid(lower), tiled_grid(middle), tiled_grid(lower), tiled_grid(source)
    )
    values_two, left_two, right_two, rows_two = partition(
        paired(rows[0], rows[4]),
        paired(rows[1], rows[5]),
        paired(rows[2], rows[6]),
        paired(rows[3], rows[7]),
    )
    head, tail = boundary_rows(tuple((entry[0] for entry in rows_two)))
    inner_ends = values_two[0] + left_two[0] * head + right_two[0] * tail
    ends = jnp.concatenate([head[None], inner_ends, tail[None]], axis=0).reshape(
        (count, 2) + shape_rest
    )
    starts = ends[:, 0]
    finishes = ends[:, 1]
    inside = value_field + left_resp * starts[:, None] + right_resp * finishes[:, None]
    merged_result = jnp.concatenate([starts[:, None], inside, finishes[:, None]], axis=1)
    return merged_result.reshape((length,) + shape_rest)


def on_device(initial_heat_state, spreading_coefficient):
    padded_margin_grid = with_halo(initial_heat_state, (("px", 1), ("py", 2)), 1)
    padded_margin_grid = jnp.pad(padded_margin_grid, ((1, 1), (0, 0), (0, 0)))
    center = padded_margin_grid[1:-1, 1:-1, 1:-1]
    neighbours = padded_margin_grid[2:, 1:-1, 1:-1] + padded_margin_grid[:-2, 1:-1, 1:-1]
    neighbours = (
        neighbours + padded_margin_grid[1:-1, 2:, 1:-1] + padded_margin_grid[1:-1, :-2, 1:-1]
    )
    neighbours = (
        neighbours + padded_margin_grid[1:-1, 1:-1, 2:] + padded_margin_grid[1:-1, 1:-1, :-2]
    )
    source = center + 0.125 * (neighbours - 6.0 * center)
    across_x = banded_linear_sweep(
        jnp.moveaxis(spreading_coefficient, 1, 0), jnp.moveaxis(source, 1, 0), interface_x
    )
    after_x = jnp.moveaxis(across_x, 0, 1)
    across_y = banded_linear_sweep(
        jnp.moveaxis(spreading_coefficient, 2, 0), jnp.moveaxis(after_x, 2, 0), boundary_rows_column
    )
    return jnp.moveaxis(across_y, 0, 2)


def solution(mesh):
    return jax.shard_map(
        on_device,
        mesh=mesh,
        in_specs=(P(None, "px", "py"), P(None, "px", "py")),
        out_specs=P(None, "px", "py"),
        check_vma=False,
    )
```

profile of v0, /device:TPU:0, one launch (start us, length us, event | category | flops | bytes accessed | tf_op | source)
XLA Modules:
  0.0 78.1 jit_solution(13411747339358266123)
XLA Ops:
  0.0 0.8 fusion.174
  0.8 2.3 %collective-permute-start = (f32[4,1,256]{2,1,0:T(1,128)S(1)}, f32[4,1,256]{2,1,0:T(1,128)S(1)}, u32[]{:S(2)}, u32[]{:S(2)}) collective-permute-start(f32[4,1,256]{2,1,0:T(1,128)S(1)} %get-tuple-element.670), channel_id=1, source_target_pairs={{0,4},{4,8},{8,12},{12,16},{16,20},{20,24},{24,28},{1,5},{5,9},{9,... | collective-permute-start | bytes 12296 | tf_op jit(solution)/shard_map/ppermute | solution.py:12
  3.1 1.3 %collective-permute-start.1 = (f32[4,1,256]{2,1,0:T(1,128)S(1)}, f32[4,1,256]{2,1,0:T(1,128)S(1)}, u32[]{:S(2)}, u32[]{:S(2)}) collective-permute-start(f32[4,1,256]{2,1,0:T(1,128)S(1)} %get-tuple-element.671), channel_id=1, source_target_pairs={{4,0},{8,4},{12,8},{16,12},{20,16},{24,20},{28,24},{5,1},{9,5},{13... | collective-permute-start | bytes 12296 | tf_op jit(solution)/shard_map/ppermute | solution.py:15
  4.4 1.2 %copy.648 = f32[4,128,256]{1,2,0:T(8,128)S(1)} copy(f32[4,128,256]{2,1,0:T(8,128)} %param.3) | data formatting | bytes 1048576 | tf_op args[1]
  5.7 0.2 fusion.107
  5.9 0.2 copy.792
  6.1 1.0 %fusion.175 = (f32[16,1,4,128]{3,1,0,2:T(1,128)}, f32[16,1,4,128]{3,1,0,2:T(1,128)S(1)}, f32[16,1,4,128]{3,1,0,2:T(1,128)S(1)}, f32[16,1,4,128]{3,1,0,2:T(1,128)...) fusion(f32[16,16,4,128]{3,1,0,2:T(8,128)S(1)} %bitcast.2309), kind=kLoop, calls=%fused_computation.1374 | loop fusion | bytes 1048576 | tf_op jit(solution)/shard_map/slice | solution.py:53
  7.1 1.1 %fusion.176 = (f32[16,1,4,128]{3,1,0,2:T(1,128)}, f32[16,1,4,128]{3,1,0,2:T(1,128)S(1)}, f32[16,1,4,128]{3,1,0,2:T(1,128)S(1)}, f32[16,1,4,128]{3,1,0,2:T(1,128)...) fusion(f32[16,16,4,128]{3,1,0,2:T(8,128)S(1)} %bitcast.2308), kind=kLoop, calls=%fused_computation.1375 | loop fusion | bytes 1048576 | tf_op jit(solution)/shard_map/slice | solution.py:52
  8.3 1.0 %constant_dynamic-update-slice_fusion.209 = (f32[16,14,4,128]{3,0,2,1:T(8,128)S(1)}, f32[16,1,4,128]{3,0,2,1:T(8,128)}, f32[16,1,4,128]{3,0,2,1:T(8,128)}, f32[1...) fusion(f32[16,1,4,128]{3,0,2,1:T(8,128)S(1)} %bitcast.2356, ...), kind=kLoop, calls=%fused_computation.236 | loop fusion | flops 868351 | bytes 2228224
  9.5 0.9 %constant_dynamic-update-slice_fusion.223 = (f32[16,14,4,128]{3,0,2,1:T(8,128)S(1)}, f32[16,1,4,128]{3,0,2,1:T(8,128)}, f32[16,1,4,128]{3,0,2,1:T(8,128)}, f32[1...) fusion(f32[16,1,4,128]{3,0,2,1:T(8,128)S(1)} %get-tuple-element, ...), kind=kLoop, calls=%fused_computation.250 | loop fusion | flops 565247 | bytes 1769472
  10.6 1.1 %fusion.171 = (f32[8,1,4,256]{3,1,0,2:T(1,128)}, f32[8,1,4,256]{3,1,0,2:T(1,128)}, f32[8,1,4,256]{3,1,0,2:T(1,128)}, f32[8,1,4,256]{3,1,0,2:T(1,128)S(1)}, f32[8...) fusion(f32[8,16,4,256]{3,1,0,2:T(8,128)S(1)} %bitcast.2310), kind=kLoop, calls=%fused_computation.1370 | loop fusion | bytes 1048576 | tf_op jit(solution)/shard_map/slice | solution.py:53
  11.8 0.2 copy.775
  12.1 0.8 %fusion.169 = (f32[4,130,1]{2,1,0:T(8,128)S(1)}, f32[4,130,1]{2,1,0:T(8,128)}) fusion(f32[4,130,256]{2,1,0:T(8,128)S(1)} %pad_maximum_fusion), kind=kLoop, calls=%fused_computation.1368 | loop fusion | bytes 8320 | tf_op jit(solution)/shard_map/slice | solution.py:15
  13.0 4.2 %collective-permute-start.2 = (f32[4,130,1]{2,1,0:T(8,128)}, f32[4,130,1]{2,1,0:T(8,128)S(1)}, u32[]{:S(2)}, u32[]{:S(2)}) collective-permute-start(f32[4,130,1]{2,1,0:T(8,128)} %get-tuple-element.601), channel_id=1, source_target_pairs={{0,1},{1,2},{2,3},{4,5},{5,6},{6,7},{8,9},{9,10},{10,11},{12,13},{... | collective-permute-start | bytes 6248 | tf_op jit(solution)/shard_map/ppermute | solution.py:12
  17.2 1.3 %collective-permute-start.3 = (f32[4,130,1]{2,1,0:T(8,128)S(1)}, f32[4,130,1]{2,1,0:T(8,128)S(1)}, u32[]{:S(2)}, u32[]{:S(2)}) collective-permute-start(f32[4,130,1]{2,1,0:T(8,128)S(1)} %get-tuple-element.600), channel_id=1, source_target_pairs={{1,0},{2,1},{3,2},{5,4},{6,5},{7,6},{9,8},{10,9},{11,10},{13,12},{... | collective-permute-start | bytes 6248 | tf_op jit(solution)/shard_map/ppermute | solution.py:15
  18.5 1.1 %fusion.173 = (f32[8,1,4,256]{3,1,0,2:T(1,128)}, f32[8,1,4,256]{3,1,0,2:T(1,128)S(1)}, f32[8,1,4,256]{3,1,0,2:T(1,128)S(1)}, f32[8,1,4,256]{3,1,0,2:T(1,128)S(1)...) fusion(f32[8,16,4,256]{3,1,0,2:T(8,128)S(1)} %bitcast.2311), kind=kLoop, calls=%fused_computation.1372 | loop fusion | bytes 1048576 | tf_op jit(solution)/shard_map/slice | solution.py:52
  19.6 3.4 %collective-permute-done.2 = f32[4,130,1]{2,1,0:T(8,128)S(1)} collective-permute-done((f32[4,130,1]{2,1,0:T(8,128)}, f32[4,130,1]{2,1,0:T(8,128)S(1)}, u32[]{:S(2)}, u32[]{:S(2)}) %collective-permute-start.2) | collective-permute-done | bytes 2112 | tf_op jit(solution)/shard_map/ppermute | solution.py:12
  22.9 7.8 %collective-permute-done.3 = f32[4,130,1]{2,1,0:T(8,128)S(1)} collective-permute-done((f32[4,130,1]{2,1,0:T(8,128)S(1)}, f32[4,130,1]{2,1,0:T(8,128)S(1)}, u32[]{:S(2)}, u32[]{:S(2)}) %collective-permute-start.3) | collective-permute-done | bytes 2112 | tf_op jit(solution)/shard_map/ppermute | solution.py:15
  30.8 0.4 select_maximum_fusion
  31.3 0.7 fusion.4
  32.0 0.4 fusion.172
  32.5 0.6 fusion.14
  33.1 0.1 multiply_divide_fusion.14
  33.3 0.1 multiply_divide_fusion.1
  33.4 0.5 copy-done.53
  34.1 0.1 constant_dynamic-update-slice_fusion.55
  34.2 0.5 copy-done.120
  35.2 0.5 copy-done.122
  35.8 0.1 subtract_divide_fusion.18
  37.7 0.2 bitcast_subtract_fusion
  38.0 0.1 bitcast_multiply_fusion.6
  38.1 0.1 bitcast_add_fusion
  38.2 0.1 fusion.58
  38.3 0.1 fusion.62
  38.6 17.7 %all_gather.6 = f32[8,8,1024]{2,0,1:T(8,128)S(1)} all-gather(f32[8,1,1024]{2,0,1:T(8,128)S(1)} %stack.78), channel_id=1, replica_groups=mesh['px'=8,'py'=4] {'px'}, dimensions={1}, use_global_device_ids=true | all-gather | bytes 294912 | tf_op jit(solution)/shard_map/all_gather | solution.py:108
  56.3 0.2 slice_bitcast_fusion.7
  57.0 0.2 slice_divide_fusion.1
  57.2 0.2 fusion.26
  57.4 0.1 multiply_subtract_fusion.142
  57.5 0.1 concatenate.44
  57.7 0.5 broadcast.238
  58.2 0.7 fusion.128
  59.0 0.1 multiply_add_fusion.2
  59.2 0.3 copy.931
  59.7 0.2 copy.932
  60.1 0.5 fusion.170
  60.8 0.1 subtract_divide_fusion.2
  61.3 0.3 copy-done.104
  61.7 0.8 %fusion.106 = (f32[16,1,4,128]{3,0,2,1:T(8,128)S(1)}, f32[16,1,4,128]{3,0,2,1:T(8,128)S(1)}, f32[16,1,4,128]{3,0,2,1:T(8,128)S(1)}, f32[16,14,4,128]{3,0,2,1:T(8...) fusion(f32[16,1,4,128]{3,0,2,1:T(8,128)S(1)} %bitcast.2398, ...), kind=kLoop, calls=%fused_computation.1363 | loop fusion | flops 98304 | bytes 524288 | tf_op jit(solution)/shard_map/mul | solution.py:54
  62.7 0.8 %constant_dynamic-update-slice_fusion.205 = (f32[16,14,4,128]{3,0,2,1:T(8,128)S(1)}, f32[16,14,4,128]{3,0,2,1:T(8,128)S(1)}, f32[16,14,4,128]{3,0,2,1:T(8,128)S(1)}) fusion(f32[16,14,4,128]{3,0,2,1:T(8,128)S(1)} %constant_dynamic-update-slice_fusion.206, f32[16,1,4,128]{3,0,2,1:T(8,128)S(1)} %copy-done.112, f32[16,1,4,128]{3,0,2,1:T(8,128)S(1)} %copy-done.10, ...), kind=kLoop, calls=%fused_computation.232 | loop fusion | flops 49152 | bytes 327680
  64.6 0.3 subtract_divide_fusion.32
  64.9 0.1 constant_dynamic-update-slice_fusion.121
  65.0 0.2 constant_dynamic-update-slice_fusion.181
  65.2 0.2 constant_dynamic-update-slice_fusion.151
  66.3 0.3 fusion.81
  66.5 0.1 multiply_divide_fusion.161
  66.7 0.1 multiply_divide_fusion.188
  66.8 0.3 constant_dynamic-update-slice_fusion.90
  67.1 0.3 constant_dynamic-update-slice_fusion.89
  67.3 0.3 constant_dynamic-update-slice_fusion.88
  67.8 8.2 %all_gather.7 = f32[8,4,512]{2,0,1:T(8,128)S(1)} all-gather(f32[8,1,512]{2,0,1:T(8,128)S(1)} %copy.980), channel_id=1, replica_groups=mesh['px'=8,'py'=4] {'py'}, dimensions={1}, use_global_device_ids=true | all-gather | bytes 81920 | tf_op jit(solution)/shard_map/all_gather | solution.py:116
  76.6 0.1 multiply_add_fusion.1
  76.8 0.3 copy.984
  77.1 1.0 %copy.985 = f32[4,128,256]{2,1,0:T(8,128)} copy(f32[4,128,256]{1,2,0:T(8,128)S(1)} %bitcast.2314) | data formatting | bytes 1048576 | tf_op jit(solution)/shard_map/transpose | solution.py:175
  (522 shorter events, 5.7 us)
Async XLA Ops:
  0.8 11.2 %collective-permute-start = (f32[4,1,256]{2,1,0:T(1,128)S(1)}, f32[4,1,256]{2,1,0:T(1,128)S(1)}, u32[]{:S(2)}, u32[]{:S(2)}) collective-permute-start(f32[4,1,256]{2,1,0:T(1,128)S(1)} %get-tuple-element.670), channel_id=1, source_target_pairs={{0,4},{4,8},{8,12},{12,16},{16,20},{20,24},{24,28},{1,5},{5,9},{9,... | collective-permute-start | bytes 12296 | tf_op jit(solution)/shard_map/ppermute | solution.py:12
  3.1 8.9 %collective-permute-start.1 = (f32[4,1,256]{2,1,0:T(1,128)S(1)}, f32[4,1,256]{2,1,0:T(1,128)S(1)}, u32[]{:S(2)}, u32[]{:S(2)}) collective-permute-start(f32[4,1,256]{2,1,0:T(1,128)S(1)} %get-tuple-element.671), channel_id=1, source_target_pairs={{4,0},{8,4},{12,8},{16,12},{20,16},{24,20},{28,24},{5,1},{9,5},{13... | collective-permute-start | bytes 12296 | tf_op jit(solution)/shard_map/ppermute | solution.py:15
  7.1 2.4 %copy-start.11 = (f32[16,1,4,128]{3,1,0,2:T(1,128)}, f32[16,1,4,128]{3,1,0,2:T(1,128)S(1)}, u32[]{:S(2)}) copy-start(f32[16,1,4,128]{3,1,0,2:T(1,128)S(1)} %get-tuple-element.673) | copy-start | bytes 98308
  8.2 2.2 %copy-start.17 = (f32[16,1,4,128]{3,1,0,2:T(1,128)}, f32[16,1,4,128]{3,1,0,2:T(1,128)S(1)}, u32[]{:S(2)}) copy-start(f32[16,1,4,128]{3,1,0,2:T(1,128)S(1)} %get-tuple-element.700) | copy-start | bytes 98308
  8.2 2.2 %copy-start.19 = (f32[16,1,4,128]{3,1,0,2:T(1,128)}, f32[16,1,4,128]{3,1,0,2:T(1,128)S(1)}, u32[]{:S(2)}) copy-start(f32[16,1,4,128]{3,1,0,2:T(1,128)S(1)} %get-tuple-element.701) | copy-start | bytes 98308
  8.2 2.2 %copy-start.21 = (f32[16,1,4,128]{3,1,0,2:T(1,128)}, f32[16,1,4,128]{3,1,0,2:T(1,128)S(1)}, u32[]{:S(2)}) copy-start(f32[16,1,4,128]{3,1,0,2:T(1,128)S(1)} %get-tuple-element.689) | copy-start | bytes 98308
  8.2 2.2 %copy-start.23 = (f32[16,1,4,128]{3,1,0,2:T(1,128)}, f32[16,1,4,128]{3,1,0,2:T(1,128)S(1)}, u32[]{:S(2)}) copy-start(f32[16,1,4,128]{3,1,0,2:T(1,128)S(1)} %get-tuple-element.690) | copy-start | bytes 98308
  8.2 2.2 %copy-start.25 = (f32[16,1,4,128]{3,1,0,2:T(1,128)}, f32[16,1,4,128]{3,1,0,2:T(1,128)S(1)}, u32[]{:S(2)}) copy-start(f32[16,1,4,128]{3,1,0,2:T(1,128)S(1)} %get-tuple-element.691) | copy-start | bytes 98308
  8.2 2.2 %copy-start.27 = (f32[16,1,4,128]{3,1,0,2:T(1,128)}, f32[16,1,4,128]{3,1,0,2:T(1,128)S(1)}, u32[]{:S(2)}) copy-start(f32[16,1,4,128]{3,1,0,2:T(1,128)S(1)} %get-tuple-element.692) | copy-start | bytes 98308
  8.2 2.2 %copy-start.29 = (f32[16,1,4,128]{3,1,0,2:T(1,128)}, f32[16,1,4,128]{3,1,0,2:T(1,128)S(1)}, u32[]{:S(2)}) copy-start(f32[16,1,4,128]{3,1,0,2:T(1,128)S(1)} %get-tuple-element.693) | copy-start | bytes 98308
  8.2 2.2 %copy-start.31 = (f32[16,1,4,128]{3,1,0,2:T(1,128)}, f32[16,1,4,128]{3,1,0,2:T(1,128)S(1)}, u32[]{:S(2)}) copy-start(f32[16,1,4,128]{3,1,0,2:T(1,128)S(1)} %get-tuple-element.694) | copy-start | bytes 98308
  8.2 2.2 %copy-start.33 = (f32[16,1,4,128]{3,1,0,2:T(1,128)}, f32[16,1,4,128]{3,1,0,2:T(1,128)S(1)}, u32[]{:S(2)}) copy-start(f32[16,1,4,128]{3,1,0,2:T(1,128)S(1)} %get-tuple-element.695) | copy-start | bytes 98308
  8.2 2.2 %copy-start.35 = (f32[16,1,4,128]{3,1,0,2:T(1,128)}, f32[16,1,4,128]{3,1,0,2:T(1,128)S(1)}, u32[]{:S(2)}) copy-start(f32[16,1,4,128]{3,1,0,2:T(1,128)S(1)} %get-tuple-element.696) | copy-start | bytes 98308
  8.2 2.2 %copy-start.37 = (f32[16,1,4,128]{3,1,0,2:T(1,128)}, f32[16,1,4,128]{3,1,0,2:T(1,128)S(1)}, u32[]{:S(2)}) copy-start(f32[16,1,4,128]{3,1,0,2:T(1,128)S(1)} %get-tuple-element.697) | copy-start | bytes 98308
  8.3 2.2 %copy-start.39 = (f32[16,1,4,128]{3,1,0,2:T(1,128)}, f32[16,1,4,128]{3,1,0,2:T(1,128)S(1)}, u32[]{:S(2)}) copy-start(f32[16,1,4,128]{3,1,0,2:T(1,128)S(1)} %get-tuple-element.698) | copy-start | bytes 98308
  8.3 2.2 %copy-start.41 = (f32[16,1,4,128]{3,1,0,2:T(1,128)}, f32[16,1,4,128]{3,1,0,2:T(1,128)S(1)}, u32[]{:S(2)}) copy-start(f32[16,1,4,128]{3,1,0,2:T(1,128)S(1)} %get-tuple-element.699) | copy-start | bytes 98308
  9.2 1.3 %copy-start.75 = (f32[16,1,4,128]{3,0,2,1:T(8,128)}, f32[16,1,4,128]{3,0,2,1:T(8,128)S(1)}, u32[]{:S(2)}) copy-start(f32[16,1,4,128]{3,0,2,1:T(8,128)S(1)} %get-tuple-element.29) | copy-start | bytes 98308
  9.2 1.3 %copy-start.77 = (f32[16,1,4,128]{3,0,2,1:T(8,128)}, f32[16,1,4,128]{3,0,2,1:T(8,128)S(1)}, u32[]{:S(2)}) copy-start(f32[16,1,4,128]{3,0,2,1:T(8,128)S(1)} %get-tuple-element.31) | copy-start | bytes 98308
  9.3 1.3 %copy-start.79 = (f32[16,1,4,128]{3,0,2,1:T(8,128)}, f32[16,1,4,128]{3,0,2,1:T(8,128)S(1)}, u32[]{:S(2)}) copy-start(f32[16,1,4,128]{3,0,2,1:T(8,128)S(1)} %get-tuple-element.33) | copy-start | bytes 98308
  9.3 1.3 %copy-start.81 = (f32[16,1,4,128]{3,0,2,1:T(8,128)}, f32[16,1,4,128]{3,0,2,1:T(8,128)S(1)}, u32[]{:S(2)}) copy-start(f32[16,1,4,128]{3,0,2,1:T(8,128)S(1)} %get-tuple-element.35) | copy-start | bytes 98308
  9.3 1.3 %copy-start.83 = (f32[16,1,4,128]{3,0,2,1:T(8,128)}, f32[16,1,4,128]{3,0,2,1:T(8,128)S(1)}, u32[]{:S(2)}) copy-start(f32[16,1,4,128]{3,0,2,1:T(8,128)S(1)} %get-tuple-element.37) | copy-start | bytes 98308
  9.3 1.3 %copy-start.85 = (f32[16,1,4,128]{3,0,2,1:T(8,128)}, f32[16,1,4,128]{3,0,2,1:T(8,128)S(1)}, u32[]{:S(2)}) copy-start(f32[16,1,4,128]{3,0,2,1:T(8,128)S(1)} %get-tuple-element.39) | copy-start | bytes 98308
  9.3 1.3 %copy-start.87 = (f32[16,1,4,128]{3,0,2,1:T(8,128)}, f32[16,1,4,128]{3,0,2,1:T(8,128)S(1)}, u32[]{:S(2)}) copy-start(f32[16,1,4,128]{3,0,2,1:T(8,128)S(1)} %get-tuple-element.41) | copy-start | bytes 98308
  9.3 1.3 %copy-start.89 = (f32[16,1,4,128]{3,0,2,1:T(8,128)}, f32[16,1,4,128]{3,0,2,1:T(8,128)S(1)}, u32[]{:S(2)}) copy-start(f32[16,1,4,128]{3,0,2,1:T(8,128)S(1)} %get-tuple-element.43) | copy-start | bytes 98308
  9.3 2.4 %copy-start.3 = (f32[16,1,4,128]{3,0,2,1:T(8,128)}, f32[16,1,4,128]{3,0,2,1:T(8,128)S(1)}, u32[]{:S(2)}) copy-start(f32[16,1,4,128]{3,0,2,1:T(8,128)S(1)} %get-tuple-element.24) | copy-start | bytes 98308
  9.3 2.4 %copy-start.5 = (f32[16,1,4,128]{3,0,2,1:T(8,128)}, f32[16,1,4,128]{3,0,2,1:T(8,128)S(1)}, u32[]{:S(2)}) copy-start(f32[16,1,4,128]{3,0,2,1:T(8,128)S(1)} %get-tuple-element.28) | copy-start | bytes 98308
  9.3 2.4 %copy-start.7 = (f32[16,1,4,128]{3,0,2,1:T(8,128)}, f32[16,1,4,128]{3,0,2,1:T(8,128)S(1)}, u32[]{:S(2)}) copy-start(f32[16,1,4,128]{3,0,2,1:T(8,128)S(1)} %get-tuple-element.32) | copy-start | bytes 98308
  9.3 2.4 %copy-start.9 = (f32[16,1,4,128]{3,0,2,1:T(8,128)}, f32[16,1,4,128]{3,0,2,1:T(8,128)S(1)}, u32[]{:S(2)}) copy-start(f32[16,1,4,128]{3,0,2,1:T(8,128)S(1)} %get-tuple-element.36) | copy-start | bytes 98308
  9.4 2.4 %copy-start.13 = (f32[16,1,4,128]{3,0,2,1:T(8,128)}, f32[16,1,4,128]{3,0,2,1:T(8,128)S(1)}, u32[]{:S(2)}) copy-start(f32[16,1,4,128]{3,0,2,1:T(8,128)S(1)} %get-tuple-element.40) | copy-start | bytes 98308
  9.4 2.4 %copy-start.15 = (f32[16,1,4,128]{3,0,2,1:T(8,128)}, f32[16,1,4,128]{3,0,2,1:T(8,128)S(1)}, u32[]{:S(2)}) copy-start(f32[16,1,4,128]{3,0,2,1:T(8,128)S(1)} %get-tuple-element.44) | copy-start | bytes 98308
  9.4 2.4 %copy-start.55 = (f32[16,1,4,128]{3,0,2,1:T(8,128)}, f32[16,1,4,128]{3,0,2,1:T(8,128)S(1)}, u32[]{:S(2)}) copy-start(f32[16,1,4,128]{3,0,2,1:T(8,128)S(1)} %get-tuple-element.21) | copy-start | bytes 98308
  9.4 2.4 %copy-start.57 = (f32[16,1,4,128]{3,0,2,1:T(8,128)}, f32[16,1,4,128]{3,0,2,1:T(8,128)S(1)}, u32[]{:S(2)}) copy-start(f32[16,1,4,128]{3,0,2,1:T(8,128)S(1)} %get-tuple-element.22) | copy-start | bytes 98308
  9.4 2.4 %copy-start.59 = (f32[16,1,4,128]{3,0,2,1:T(8,128)}, f32[16,1,4,128]{3,0,2,1:T(8,128)S(1)}, u32[]{:S(2)}) copy-start(f32[16,1,4,128]{3,0,2,1:T(8,128)S(1)} %get-tuple-element.26) | copy-start | bytes 98308
  9.4 2.4 %copy-start.61 = (f32[16,1,4,128]{3,0,2,1:T(8,128)}, f32[16,1,4,128]{3,0,2,1:T(8,128)S(1)}, u32[]{:S(2)}) copy-start(f32[16,1,4,128]{3,0,2,1:T(8,128)S(1)} %get-tuple-element.30) | copy-start | bytes 98308
  9.4 2.4 %copy-start.63 = (f32[16,1,4,128]{3,0,2,1:T(8,128)}, f32[16,1,4,128]{3,0,2,1:T(8,128)S(1)}, u32[]{:S(2)}) copy-start(f32[16,1,4,128]{3,0,2,1:T(8,128)S(1)} %get-tuple-element.34) | copy-start | bytes 98308
  9.4 2.4 %copy-start.65 = (f32[16,1,4,128]{3,0,2,1:T(8,128)}, f32[16,1,4,128]{3,0,2,1:T(8,128)S(1)}, u32[]{:S(2)}) copy-start(f32[16,1,4,128]{3,0,2,1:T(8,128)S(1)} %get-tuple-element.38) | copy-start | bytes 98308
  9.4 2.4 %copy-start.67 = (f32[16,1,4,128]{3,0,2,1:T(8,128)}, f32[16,1,4,128]{3,0,2,1:T(8,128)S(1)}, u32[]{:S(2)}) copy-start(f32[16,1,4,128]{3,0,2,1:T(8,128)S(1)} %get-tuple-element.42) | copy-start | bytes 98308
  9.4 2.4 %copy-start.69 = (f32[16,1,4,128]{3,0,2,1:T(8,128)}, f32[16,1,4,128]{3,0,2,1:T(8,128)S(1)}, u32[]{:S(2)}) copy-start(f32[16,1,4,128]{3,0,2,1:T(8,128)S(1)} %get-tuple-element.23) | copy-start | bytes 98308
  9.5 2.4 %copy-start.71 = (f32[16,1,4,128]{3,0,2,1:T(8,128)}, f32[16,1,4,128]{3,0,2,1:T(8,128)S(1)}, u32[]{:S(2)}) copy-start(f32[16,1,4,128]{3,0,2,1:T(8,128)S(1)} %get-tuple-element.25) | copy-start | bytes 98308
  10.6 1.4 %copy-start = (f32[4,128,256]{2,1,0:T(8,128)S(1)}, f32[4,128,256]{2,1,0:T(8,128)}, u32[]{:S(2)}) copy-start(f32[4,128,256]{2,1,0:T(8,128)} %param.2) | copy-start | bytes 1572868
  13.0 10.0 %collective-permute-start.2 = (f32[4,130,1]{2,1,0:T(8,128)}, f32[4,130,1]{2,1,0:T(8,128)S(1)}, u32[]{:S(2)}, u32[]{:S(2)}) collective-permute-start(f32[4,130,1]{2,1,0:T(8,128)} %get-tuple-element.601), channel_id=1, source_target_pairs={{0,1},{1,2},{2,3},{4,5},{5,6},{6,7},{8,9},{9,10},{10,11},{12,13},{... | collective-permute-start | bytes 6248 | tf_op jit(solution)/shard_map/ppermute | solution.py:12
  17.2 13.6 %collective-permute-start.3 = (f32[4,130,1]{2,1,0:T(8,128)S(1)}, f32[4,130,1]{2,1,0:T(8,128)S(1)}, u32[]{:S(2)}, u32[]{:S(2)}) collective-permute-start(f32[4,130,1]{2,1,0:T(8,128)S(1)} %get-tuple-element.600), channel_id=1, source_target_pairs={{1,0},{2,1},{3,2},{5,4},{6,5},{7,6},{9,8},{10,9},{11,10},{13,12},{... | collective-permute-start | bytes 6248 | tf_op jit(solution)/shard_map/ppermute | solution.py:15
  60.9 1.6 %copy-start.100 = (f32[16,1,4,128]{3,0,2,1:T(8,128)S(1)}, f32[16,1,4,128]{3,0,2,1:T(8,128)}, u32[]{:S(2)}) copy-start(f32[16,1,4,128]{3,0,2,1:T(8,128)} %get-tuple-element.7) | copy-start | bytes 98308
  60.9 1.6 %copy-start.102 = (f32[16,1,4,128]{3,0,2,1:T(8,128)S(1)}, f32[16,1,4,128]{3,0,2,1:T(8,128)}, u32[]{:S(2)}) copy-start(f32[16,1,4,128]{3,0,2,1:T(8,128)} %get-tuple-element.56) | copy-start | bytes 98308
  60.9 1.6 %copy-start.114 = (f32[16,1,4,128]{3,0,2,1:T(8,128)S(1)}, f32[16,1,4,128]{3,0,2,1:T(8,128)}, u32[]{:S(2)}) copy-start(f32[16,1,4,128]{3,0,2,1:T(8,128)} %get-tuple-element.19) | copy-start | bytes 98308
  61.0 1.6 %copy-start.117 = (f32[16,1,4,128]{3,0,2,1:T(8,128)S(1)}, f32[16,1,4,128]{3,0,2,1:T(8,128)}, u32[]{:S(2)}) copy-start(f32[16,1,4,128]{3,0,2,1:T(8,128)} %get-tuple-element.67) | copy-start | bytes 98308
  61.0 1.7 %copy-start.98 = (f32[16,1,4,128]{3,0,2,1:T(8,128)S(1)}, f32[16,1,4,128]{3,0,2,1:T(8,128)}, u32[]{:S(2)}) copy-start(f32[16,1,4,128]{3,0,2,1:T(8,128)} %get-tuple-element.8) | copy-start | bytes 98308
  61.0 1.7 %copy-start.101 = (f32[16,1,4,128]{3,0,2,1:T(8,128)S(1)}, f32[16,1,4,128]{3,0,2,1:T(8,128)}, u32[]{:S(2)}) copy-start(f32[16,1,4,128]{3,0,2,1:T(8,128)} %get-tuple-element.57) | copy-start | bytes 98308
  61.0 1.7 %copy-start.112 = (f32[16,1,4,128]{3,0,2,1:T(8,128)S(1)}, f32[16,1,4,128]{3,0,2,1:T(8,128)}, u32[]{:S(2)}) copy-start(f32[16,1,4,128]{3,0,2,1:T(8,128)} %get-tuple-element.18) | copy-start | bytes 98308
  61.2 2.4 %copy-start.95 = (f32[16,1,4,128]{3,0,2,1:T(8,128)S(1)}, f32[16,1,4,128]{3,0,2,1:T(8,128)}, u32[]{:S(2)}) copy-start(f32[16,1,4,128]{3,0,2,1:T(8,128)} %get-tuple-element.9) | copy-start | bytes 98308
  61.2 2.4 %copy-start.99 = (f32[16,1,4,128]{3,0,2,1:T(8,128)S(1)}, f32[16,1,4,128]{3,0,2,1:T(8,128)}, u32[]{:S(2)}) copy-start(f32[16,1,4,128]{3,0,2,1:T(8,128)} %get-tuple-element.58) | copy-start | bytes 98308
  61.2 2.4 %copy-start.110 = (f32[16,1,4,128]{3,0,2,1:T(8,128)S(1)}, f32[16,1,4,128]{3,0,2,1:T(8,128)}, u32[]{:S(2)}) copy-start(f32[16,1,4,128]{3,0,2,1:T(8,128)} %get-tuple-element.17) | copy-start | bytes 98308
  61.2 2.4 %copy-start.113 = (f32[16,1,4,128]{3,0,2,1:T(8,128)S(1)}, f32[16,1,4,128]{3,0,2,1:T(8,128)}, u32[]{:S(2)}) copy-start(f32[16,1,4,128]{3,0,2,1:T(8,128)} %get-tuple-element.65) | copy-start | bytes 98308
  61.3 2.4 %copy-start.94 = (f32[16,1,4,128]{3,0,2,1:T(8,128)S(1)}, f32[16,1,4,128]{3,0,2,1:T(8,128)}, u32[]{:S(2)}) copy-start(f32[16,1,4,128]{3,0,2,1:T(8,128)} %get-tuple-element.10) | copy-start | bytes 98308
  61.3 2.4 %copy-start.97 = (f32[16,1,4,128]{3,0,2,1:T(8,128)S(1)}, f32[16,1,4,128]{3,0,2,1:T(8,128)}, u32[]{:S(2)}) copy-start(f32[16,1,4,128]{3,0,2,1:T(8,128)} %get-tuple-element.59) | copy-start | bytes 98308
  61.3 2.4 %copy-start.108 = (f32[16,1,4,128]{3,0,2,1:T(8,128)S(1)}, f32[16,1,4,128]{3,0,2,1:T(8,128)}, u32[]{:S(2)}) copy-start(f32[16,1,4,128]{3,0,2,1:T(8,128)} %get-tuple-element.16) | copy-start | bytes 98308
  61.3 2.4 %copy-start.111 = (f32[16,1,4,128]{3,0,2,1:T(8,128)S(1)}, f32[16,1,4,128]{3,0,2,1:T(8,128)}, u32[]{:S(2)}) copy-start(f32[16,1,4,128]{3,0,2,1:T(8,128)} %get-tuple-element.64) | copy-start | bytes 98308
  61.7 2.1 %copy-start.93 = (f32[16,1,4,128]{3,0,2,1:T(8,128)S(1)}, f32[16,1,4,128]{3,0,2,1:T(8,128)}, u32[]{:S(2)}) copy-start(f32[16,1,4,128]{3,0,2,1:T(8,128)} %get-tuple-element.11) | copy-start | bytes 98308
  61.7 2.1 %copy-start.96 = (f32[16,1,4,128]{3,0,2,1:T(8,128)S(1)}, f32[16,1,4,128]{3,0,2,1:T(8,128)}, u32[]{:S(2)}) copy-start(f32[16,1,4,128]{3,0,2,1:T(8,128)} %get-tuple-element.60) | copy-start | bytes 98308
  61.7 2.1 %copy-start.106 = (f32[16,1,4,128]{3,0,2,1:T(8,128)S(1)}, f32[16,1,4,128]{3,0,2,1:T(8,128)}, u32[]{:S(2)}) copy-start(f32[16,1,4,128]{3,0,2,1:T(8,128)} %get-tuple-element.15) | copy-start | bytes 98308
  61.7 2.1 %copy-start.109 = (f32[16,1,4,128]{3,0,2,1:T(8,128)S(1)}, f32[16,1,4,128]{3,0,2,1:T(8,128)}, u32[]{:S(2)}) copy-start(f32[16,1,4,128]{3,0,2,1:T(8,128)} %get-tuple-element.63) | copy-start | bytes 98308
  62.6 1.3 %copy-start.91 = (f32[16,1,4,128]{3,0,2,1:T(8,128)S(1)}, f32[16,1,4,128]{3,0,2,1:T(8,128)}, u32[]{:S(2)}) copy-start(f32[16,1,4,128]{3,0,2,1:T(8,128)} %get-tuple-element.12) | copy-start | bytes 98308
  62.6 1.3 %copy-start.92 = (f32[16,1,4,128]{3,0,2,1:T(8,128)S(1)}, f32[16,1,4,128]{3,0,2,1:T(8,128)}, u32[]{:S(2)}) copy-start(f32[16,1,4,128]{3,0,2,1:T(8,128)} %get-tuple-element.61) | copy-start | bytes 98308
  62.6 1.3 %copy-start.105 = (f32[16,1,4,128]{3,0,2,1:T(8,128)S(1)}, f32[16,1,4,128]{3,0,2,1:T(8,128)}, u32[]{:S(2)}) copy-start(f32[16,1,4,128]{3,0,2,1:T(8,128)} %get-tuple-element.14) | copy-start | bytes 98308
  (64 other events, 68.3 us)
where the time goes:
time: 78.8 us; the launch traced here: 78.1 us
  blocking collectives  25.9 us (33%)
  local copies, waits for them, and re-layouts  16.8 us (21%)
  other arithmetic  11.8 us (15%)
  waiting for transfers between devices  11.2 us (14%)
  starting transfers between devices  9.16 us (12%)
  between operations  3.16 us (4%)
    all_gather x1, blocking collectives, interface_x(): whole = lax.all_gather(piled_arrays[:, None], 'px', axis=1, tiled=True)  17.7 us
    all_gather x1, blocking collectives, boundary_rows_column(): whole = lax.all_gather(piled_arrays[:, None], 'py', axis=1, tiled=True)  8.22 us
    ppermute x2, waiting for transfers between devices, with_halo(): lax.ppermute(lax.slice_in_dim(block, 0, width, axis=dim), axis, backward)  7.81 us
    ppermute x2, starting transfers between devices, with_halo(): lax.ppermute(lax.slice_in_dim(block, block.shape[dim] - width, None, axis...  6.57 us
    unnamed x50, other arithmetic  5.29 us
    unnamed x343, local copies, waits for them, and re-layouts  4.3 us
    ppermute x2, waiting for transfers between devices, with_halo(): lax.ppermute(lax.slice_in_dim(block, block.shape[dim] - width, None, axis...  3.38 us
    ppermute x2, starting transfers between devices, with_halo(): lax.ppermute(lax.slice_in_dim(block, 0, width, axis=dim), axis, backward)  2.58 us
  transfers between devices with their start and end apart: 4, of which 2 were waited for; matrix products, arithmetic and copies ran while one was open for 10% of the time, Pallas kernels for 0%

commit v1 on v0

v1 whole, which is shorter than its diff:
```python
import functools

import jax
import jax.numpy as jnp
from jax import lax
from jax.experimental import pallas as pl
from jax.experimental.pallas import tpu as pltpu
from jax.sharding import PartitionSpec as P

LANES = 128
BLOCKS = 8
MESH = pl.DeviceIdType.MESH


def combine(left, right):
    e_p, w_p, a_p = left
    e_q, w_q, a_q = right
    gap_p = e_p + w_p
    gap_q = e_q + a_q
    r_p = 1.0 - gap_p
    b_q = 1.0 - gap_q
    inv = 1.0 / (gap_p + r_p * gap_q)
    joined = (
        e_p * e_q * inv,
        w_q + e_q * ((w_p + r_p * a_q) * inv),
        a_p + e_p * ((a_q + b_q * w_p) * inv),
    )
    return joined, (inv, r_p, b_q, e_p, e_q)


def combine_rhs(node, left, right):
    inv, r_p, b_q, e_p, e_q = node
    u_p, a_p = left
    u_q, a_q = right
    p0 = (u_p + r_p * a_q) * inv
    q0 = (a_q + b_q * u_p) * inv
    return (u_q + e_q * p0, a_p + e_p * q0), (p0, q0)


def split(node, start, low, high):
    inv, r_p, b_q, e_p, e_q = node
    p0, q0 = start
    from_low = e_p * inv * low
    from_high = e_q * inv * high
    p = p0 + from_low + r_p * from_high
    q = q0 + b_q * from_low + from_high
    return p, q


def tree_coefficients(leaves):
    nodes = []
    while len(leaves) > 1:
        pairs = [combine(leaves[i], leaves[i + 1]) for i in range(0, len(leaves), 2)]
        leaves = [pair[0] for pair in pairs]
        nodes.append([pair[1] for pair in pairs])
    return leaves[0], nodes


def tree_up(nodes, leaves):
    starts = []
    for level in nodes:
        pairs = [
            combine_rhs(level[i], leaves[2 * i], leaves[2 * i + 1]) for i in range(len(level))
        ]
        leaves = [pair[0] for pair in pairs]
        starts.append([pair[1] for pair in pairs])
    return leaves[0], starts


def tree_down(nodes, starts, low, high):
    bounds = [(low, high)]
    for level, begin in zip(reversed(nodes), reversed(starts)):
        below = []
        for i, (lo, hi) in enumerate(bounds):
            p, q = split(level[i], begin[i], lo, hi)
            below += [(lo, q), (p, hi)]
        bounds = below
    return bounds


def leaf_rows(turn_ref, values, count):
    turn_ref[0 : count * BLOCKS, :] = values.reshape(count * BLOCKS, LANES)
    return [turn_ref[pl.ds(b, count, stride=BLOCKS), :] for b in range(BLOCKS)]


def block_rows(turn_ref, rows, count):
    for b in range(BLOCKS):
        turn_ref[pl.ds(b, count, stride=BLOCKS), :] = rows[b]
    return turn_ref[0 : count * BLOCKS, :].reshape(count, BLOCKS, LANES)


def sweep_coefficients(m_ref, r_ref, e_ref, turn_refs, length):
    count = m_ref.shape[0]
    for g in range(length):
        m = m_ref[:, pl.ds(g, BLOCKS, stride=length), :]
        if g == 0:
            t = 1.0 + m
            r = 1.0 / (1.0 + t)
            e = r
            w = m * r
            a = w
        else:
            t = m + t * r
            r = 1.0 / (1.0 + t)
            w = (m + w) * r
            a = a + e * w
            e = e * r
        r_ref[g] = r
        e_ref[g] = e
    leaves = [leaf_rows(ref, value, count) for ref, value in zip(turn_refs, (e, w, a))]
    return tree_coefficients([tuple(leaf[b] for leaf in leaves) for b in range(BLOCKS)])


def chain_coefficients(gathered, count):
    blocks = [tuple(gathered[i, c] for c in range(3)) for i in range(count)]
    total, nodes = blocks[0], []
    for i in range(1, count):
        total, node = combine(total, blocks[i])
        nodes.append(node)
    return nodes


def chain_solve(nodes, gathered, last_ref, first_ref, count):
    u = [gathered[i, 0] for i in range(count)]
    a = [gathered[i, 1] for i in range(count)]
    zero = jnp.zeros_like(u[0])
    state = (u[0], zero)
    starts = []
    for i in range(1, count):
        state, start = combine_rhs(nodes[i - 1], state, (u[i], a[i]))
        starts.append(start)
    last_ref[0] = zero
    first_ref[count - 1] = zero
    high = zero
    for i in range(count - 1, 0, -1):
        p, q = split(nodes[i - 1], starts[i - 1], zero, high)
        last_ref[i] = p
        first_ref[i - 1] = q
        high = q


def kernel(
    nx,
    ny,
    h_ref,
    k_ref,
    out_ref,
    m_ref,
    mt_ref,
    rx_ref,
    ex_ref,
    ux_ref,
    ry_ref,
    ey_ref,
    uy_ref,
    mid_ref,
    midt_ref,
    turn0,
    turn1,
    turn2,
    hxs_ref,
    hxr_ref,
    hys_ref,
    hyr_ref,
    col_ref,
    cgx,
    rgx,
    cgy,
    rgy,
    lastx,
    firstx,
    lasty,
    firsty,
    hs_sem,
    hr_sem,
    csx,
    crx,
    rsx,
    rrx,
    csy,
    cry,
    rsy,
    rry,
):
    ix = lax.axis_index("px")
    iy = lax.axis_index("py")
    planes, rows, columns = h_ref.shape
    tiles = columns // LANES
    lx = rows // BLOCKS
    ly = columns // BLOCKS
    turns = (turn0, turn1, turn2)

    barrier = pltpu.get_barrier_semaphore()
    for d in range(1, nx):
        pl.semaphore_signal(
            barrier, inc=1, device_id=(lax.rem(ix + d, nx), iy), device_id_type=MESH
        )
    for d in range(1, ny):
        pl.semaphore_signal(
            barrier, inc=1, device_id=(ix, lax.rem(iy + d, ny)), device_id_type=MESH
        )

    def peers_x(ref, send, recv):
        return [
            pltpu.make_async_remote_copy(
                src_ref=ref.at[ix],
                dst_ref=ref.at[ix],
                send_sem=send.at[d - 1],
                recv_sem=recv.at[d - 1],
                device_id=(lax.rem(ix + d, nx), iy),
                device_id_type=MESH,
            )
            for d in range(1, nx)
        ]

    def peers_y(ref, send, recv):
        return [
            pltpu.make_async_remote_copy(
                src_ref=ref.at[iy],
                dst_ref=ref.at[iy],
                send_sem=send.at[d - 1],
                recv_sem=recv.at[d - 1],
                device_id=(ix, lax.rem(iy + d, ny)),
                device_id_type=MESH,
            )
            for d in range(1, ny)
        ]

    for j in range(tiles):
        at = pl.ds(j * LANES, LANES)
        part = pl.ds(j * planes, planes)
        hxs_ref[0, part] = h_ref[:, 0, at]
        hxs_ref[1, part] = h_ref[:, rows - 1, at]
    lane = lax.broadcasted_iota(jnp.int32, (rows, LANES), 1)
    packed = jnp.zeros((rows, LANES), jnp.float32)
    for p in range(planes):
        low = h_ref[p, :, 0:LANES]
        high = h_ref[p, :, columns - LANES : columns]
        packed = jnp.where(lane == p, low if p == 0 else pltpu.roll(low, p, 1), packed)
        packed = jnp.where(lane == planes + p, pltpu.roll(high, planes + p + 1, 1), packed)
    edge = packed.T
    hys_ref[0] = edge[0:planes]
    hys_ref[1] = edge[planes : 2 * planes]

    @pl.when(ix == 0)
    def _():
        hxr_ref[1] = jnp.zeros_like(hxr_ref[1])

    @pl.when(ix == nx - 1)
    def _():
        hxr_ref[0] = jnp.zeros_like(hxr_ref[0])

    @pl.when(iy == 0)
    def _():
        hyr_ref[1] = jnp.zeros_like(hyr_ref[1])

    @pl.when(iy == ny - 1)
    def _():
        hyr_ref[0] = jnp.zeros_like(hyr_ref[0])

    def halo(source, target, slot, number, device):
        return pltpu.make_async_remote_copy(
            src_ref=source.at[slot],
            dst_ref=target.at[slot],
            send_sem=hs_sem.at[number],
            recv_sem=hr_sem.at[number],
            device_id=device,
            device_id_type=MESH,
        )

    x_down = halo(hxs_ref, hxr_ref, 0, 0, (lax.rem(ix + nx - 1, nx), iy))
    x_up = halo(hxs_ref, hxr_ref, 1, 1, (lax.rem(ix + 1, nx), iy))
    y_down = halo(hys_ref, hyr_ref, 0, 2, (ix, lax.rem(iy + ny - 1, ny)))
    y_up = halo(hys_ref, hyr_ref, 1, 3, (ix, lax.rem(iy + 1, ny)))
    routes = (
        (x_down, ix > 0, ix < nx - 1),
        (x_up, ix < nx - 1, ix > 0),
        (y_down, iy > 0, iy < ny - 1),
        (y_up, iy < ny - 1, iy > 0),
    )

    pl.semaphore_wait(barrier, nx + ny - 2)
    for copy, sends, _ in routes:
        pl.when(sends)(copy.start)

    for j in range(tiles):
        mid_ref[pl.ds(j * planes, planes)] = h_ref[:, :, pl.ds(j * LANES, LANES)]
        m_ref[pl.ds(j * planes, planes)] = 1.0 / k_ref[:, :, pl.ds(j * LANES, LANES)]
    joined, nodes_x = sweep_coefficients(m_ref, rx_ref, ex_ref, turns, lx)
    for c in range(3):
        cgx[ix, c] = joined[c]
    send_cx = peers_x(cgx, csx, crx)
    for copy in send_cx:
        copy.start()
    for p in range(planes):
        for j in range(tiles):
            mt_ref[p, pl.ds(j * LANES, LANES), :] = m_ref[j * planes + p].T
    joined, nodes_y = sweep_coefficients(mt_ref, ry_ref, ey_ref, turns, ly)
    for c in range(3):
        cgy[iy, c] = joined[c]
    send_cy = peers_y(cgy, csy, cry)
    for copy in send_cy:
        copy.start()

    for copy, _, receives in routes:
        pl.when(receives)(copy.wait_recv)
    spread = jnp.concatenate(
        [hyr_ref[1], hyr_ref[0], jnp.zeros((LANES - 2 * planes, LANES), jnp.float32)], axis=0
    )
    col_ref[...] = spread.T

    def field(g):
        return mid_ref[:, pl.ds(g, BLOCKS, stride=lx), :]

    count = tiles * planes
    shape = (count, BLOCKS, LANES)
    sub = lax.broadcasted_iota(jnp.int32, shape, 1)
    lane1 = lax.broadcasted_iota(jnp.int32, (BLOCKS, LANES), 1)
    none = jnp.zeros((BLOCKS, LANES), jnp.float32)
    now = field(0)
    before = jnp.where(sub == 0, hxr_ref[1][:, None, :], pltpu.roll(field(lx - 1), 1, 1))
    beyond = jnp.where(sub == BLOCKS - 1, hxr_ref[0][:, None, :], pltpu.roll(now, BLOCKS - 1, 1))
    u = jnp.zeros(shape, jnp.float32)
    total = jnp.zeros(shape, jnp.float32)
    for g in range(lx):
        after = field(g + 1) if g + 1 < lx else beyond
        to_right = pltpu.roll(now, 1, 2)
        to_left = pltpu.roll(now, LANES - 1, 2)
        column = col_ref[pl.ds(g, BLOCKS, stride=lx), :]
        around = []
        for j in range(tiles):
            for p in range(planes):
                i = j * planes + p
                if j == 0:
                    low = column if p == 0 else pltpu.roll(column, LANES - p, 1)
                else:
                    low = to_right[i - planes]
                if j == tiles - 1:
                    high = pltpu.roll(column, LANES - 1 - planes - p, 1)
                else:
                    high = to_left[i + planes]
                left = jnp.where(lane1 == 0, low, to_right[i])
                right = jnp.where(lane1 == LANES - 1, high, to_left[i])
                under = now[i - 1] if p > 0 else none
                over = now[i + 1] if p < planes - 1 else none
                around.append((over + under) + (left + right))
        around = jnp.stack(around) + (after + before)
        source = now + 0.125 * (around - 6.0 * now)
        m = m_ref[:, pl.ds(g, BLOCKS, stride=lx), :]
        u = (source * m + u) * rx_ref[g]
        total = u if g == 0 else total + ex_ref[g - 1] * u
        ux_ref[g] = u
        before, now = now, after

    def finish_sweep(u, total, nodes, count, length, r_ref, e_ref, u_ref, store, exchange):
        leaves = [leaf_rows(ref, value, count) for ref, value in zip(turns, (u, total))]
        (u_top, a_top), starts = tree_up(nodes, list(zip(*leaves)))
        low, high = exchange(u_top, a_top)
        bounds = tree_down(nodes, starts, low, high)
        low = block_rows(turn0, [b[0] for b in bounds], count)
        value = block_rows(turn1, [b[1] for b in bounds], count)
        for g in range(length - 1, -1, -1):
            value = (u_ref[g] + e_ref[g] * low) + r_ref[g] * value
            store(g, value)

    def exchange_x(u_top, a_top):
        rgx[ix, 0] = u_top
        rgx[ix, 1] = a_top
        send = peers_x(rgx, rsx, rrx)
        for copy in send:
            copy.start()
        for copy in send_cx:
            copy.wait()
        chain = chain_coefficients(cgx, nx)
        for copy in send:
            copy.wait()
        chain_solve(chain, rgx, lastx, firstx, nx)
        return lastx[ix], firstx[ix]

    def exchange_y(u_top, a_top):
        rgy[iy, 0] = u_top
        rgy[iy, 1] = a_top
        send = peers_y(rgy, rsy, rry)
        for copy in send:
            copy.start()
        for copy in send_cy:
            copy.wait()
        chain = chain_coefficients(cgy, ny)
        for copy in send:
            copy.wait()
        chain_solve(chain, rgy, lasty, firsty, ny)
        return lasty[iy], firsty[iy]

    def store_x(g, value):
        mid_ref[:, pl.ds(g, BLOCKS, stride=lx), :] = value

    finish_sweep(u, total, nodes_x, count, lx, rx_ref, ex_ref, ux_ref, store_x, exchange_x)

    for p in range(planes):
        for j in range(tiles):
            midt_ref[p, pl.ds(j * LANES, LANES), :] = mid_ref[j * planes + p].T
    u = jnp.zeros((planes, BLOCKS, LANES), jnp.float32)
    total = u
    for g in range(ly):
        source = midt_ref[:, pl.ds(g, BLOCKS, stride=ly), :]
        m = mt_ref[:, pl.ds(g, BLOCKS, stride=ly), :]
        u = (source * m + u) * ry_ref[g]
        total = u if g == 0 else total + ey_ref[g - 1] * u
        uy_ref[g] = u

    def store_y(g, value):
        midt_ref[:, pl.ds(g, BLOCKS, stride=ly), :] = value

    finish_sweep(u, total, nodes_y, planes, ly, ry_ref, ey_ref, uy_ref, store_y, exchange_y)
    for p in range(planes):
        for j in range(tiles):
            at = pl.ds(j * LANES, LANES)
            out_ref[p, :, at] = midt_ref[p, at, :].T
    for copy, sends, _ in routes:
        pl.when(sends)(copy.wait_send)


def on_device(nx, ny, initial_heat_state, spreading_coefficient):
    planes, rows, columns = initial_heat_state.shape
    count = planes * (columns // LANES)
    lx = rows // BLOCKS
    ly = columns // BLOCKS

    def vmem(*shape):
        return pltpu.VMEM(shape, jnp.float32)

    def dma(number):
        return pltpu.SemaphoreType.DMA((number,))

    return pl.pallas_call(
        functools.partial(kernel, nx, ny),
        out_shape=jax.ShapeDtypeStruct((planes, rows, columns), jnp.float32),
        in_specs=[pl.BlockSpec(memory_space=pltpu.VMEM)] * 2,
        out_specs=pl.BlockSpec(memory_space=pltpu.VMEM),
        scratch_shapes=[
            vmem(count, rows, LANES),
            vmem(planes, columns, LANES),
            vmem(lx, count, BLOCKS, LANES),
            vmem(lx, count, BLOCKS, LANES),
            vmem(lx, count, BLOCKS, LANES),
            vmem(ly, planes, BLOCKS, LANES),
            vmem(ly, planes, BLOCKS, LANES),
            vmem(ly, planes, BLOCKS, LANES),
            vmem(count, rows, LANES),
            vmem(planes, columns, LANES),
            vmem(count * BLOCKS, LANES),
            vmem(count * BLOCKS, LANES),
            vmem(count * BLOCKS, LANES),
            vmem(2, count, LANES),
            vmem(2, count, LANES),
            vmem(2, planes, LANES),
            vmem(2, planes, LANES),
            vmem(rows, LANES),
            vmem(nx, 3, count, LANES),
            vmem(nx, 2, count, LANES),
            vmem(ny, 3, planes, LANES),
            vmem(ny, 2, planes, LANES),
            vmem(nx, count, LANES),
            vmem(nx, count, LANES),
            vmem(ny, planes, LANES),
            vmem(ny, planes, LANES),
            dma(4),
            dma(4),
            dma(nx - 1),
            dma(nx - 1),
            dma(nx - 1),
            dma(nx - 1),
            dma(ny - 1),
            dma(ny - 1),
            dma(ny - 1),
            dma(ny - 1),
        ],
        compiler_params=pltpu.CompilerParams(
            collective_id=0, has_side_effects=True, vmem_limit_bytes=32 << 20
        ),
    )(initial_heat_state, spreading_coefficient)


def solution(mesh):
    return jax.shard_map(
        functools.partial(on_device, mesh.shape["px"], mesh.shape["py"]),
        mesh=mesh,
        in_specs=(P(None, "px", "py"), P(None, "px", "py")),
        out_specs=P(None, "px", "py"),
        check_vma=False,
    )
```

time: 78.8 us -> 20.3 us (0.26)
  blocking collectives: 25.9 us -> 0 us
  Pallas kernels: 0 us -> 17.2 us
  local copies, waits for them, and re-layouts: 16.8 us -> 2.88 us
  other arithmetic: 11.8 us -> 0 us
  waiting for transfers between devices: 11.2 us -> 0 us
  starting transfers between devices: 9.16 us -> 0 us
  between operations: 3.16 us -> 0.01 us
    all_gather x2 -> x0, blocking collectives: 25.9 us -> none  [the longest x1 17.7 us: interface_x(): whole = lax.all_gather(piled_arrays[:, None], 'px', axis=1, tiled=True)]
    pallas_call x0 -> x1, Pallas kernels: none -> 17.2 us  [on_device(): pl.pallas_call(functools.partial(kernel, nx, ny), out_shape=jax.ShapeDtyp...]
    ppermute x4 -> x0, waiting for transfers between devices: 11.2 us -> none  [the longest x2 7.81 us: with_halo(): lax.ppermute(lax.slice_in_dim(block, 0, width, axis=dim), axis, backward)]
    ppermute x4 -> x0, starting transfers between devices: 9.16 us -> none  [the longest x2 6.57 us: with_halo(): lax.ppermute(lax.slice_in_dim(block, block.shape[dim] - width, None, axis...]
    slice x24 -> x0, local copies, waits for them, and re-layouts: 8.2 us -> none  [the longest x2 2.13 us: partition(): lower[:, 0]]
    unnamed x50 -> x0, other arithmetic: 5.29 us -> none
    div x14 -> x0, other arithmetic: 2.49 us -> none  [the longest x5 1.45 us: partition(): value_field.append(value_num / divisor)]
    unnamed x343 -> x5, local copies, waits for them, and re-layouts: 4.3 us -> 2.88 us
  transfers between devices with their start and end apart: 4 -> 0, of which waited for: 2 -> 0; matrix products, arithmetic and copies ran while one was open for 10% -> 0% of each run, Pallas kernels for 0% -> 0%
where the time goes in v1:
time: 20.3 us; the launch traced here: 20.1 us
  Pallas kernels  17.2 us (85%)
  local copies, waits for them, and re-layouts  2.88 us (14%)
    pallas_call x1, Pallas kernels, on_device(): pl.pallas_call(functools.partial(kernel, nx, ny), out_shape=jax.ShapeDtyp...  17.2 us
    unnamed x5, local copies, waits for them, and re-layouts  2.88 us

profile of v1, /device:TPU:0, one launch (start us, length us, event | category | flops | bytes accessed | tf_op | source)
XLA Modules:
  0.0 20.1 jit_solution(13483687770601785425)
XLA Ops:
  0.0 0.0 copy-start
  0.0 1.0 %copy-done = f32[4,128,256]{2,1,0:T(8,128)S(1)} copy-done((f32[4,128,256]{2,1,0:T(8,128)S(1)}, f32[4,128,256]{2,1,0:T(8,128)}, u32[]{:S(2)}) %copy-start) | copy-done | bytes 524312
  1.0 0.0 copy-start.1
  1.0 1.0 %copy-done.1 = f32[4,128,256]{2,1,0:T(8,128)S(1)} copy-done((f32[4,128,256]{2,1,0:T(8,128)S(1)}, f32[4,128,256]{2,1,0:T(8,128)}, u32[]{:S(2)}) %copy-start.1) | copy-done | bytes 524312
  2.1 17.2 %shard_map.28 = f32[4,128,256]{2,1,0:T(8,128)S(1)} custom-call(f32[4,128,256]{2,1,0:T(8,128)S(1)} %copy-done, f32[4,128,256]{2,1,0:T(8,128)S(1)} %copy-done.1), custom_call_target="tpu_custom_call" | custom-call | tf_op jit(solution)/shard_map/pallas_call | solution.py:435
  19.3 0.8 %copy.4 = f32[4,128,256]{2,1,0:T(8,128)} copy(f32[4,128,256]{2,1,0:T(8,128)S(1)} %shard_map.28) | data formatting | bytes 1048576
Async XLA Ops:
  0.0 1.0 %copy-start = (f32[4,128,256]{2,1,0:T(8,128)S(1)}, f32[4,128,256]{2,1,0:T(8,128)}, u32[]{:S(2)}) copy-start(f32[4,128,256]{2,1,0:T(8,128)} %h_ref.1) | copy-start | bytes 1572868
  1.0 1.0 %copy-start.1 = (f32[4,128,256]{2,1,0:T(8,128)S(1)}, f32[4,128,256]{2,1,0:T(8,128)}, u32[]{:S(2)}) copy-start(f32[4,128,256]{2,1,0:T(8,128)} %k_ref.1) | copy-start | bytes 1572868

commit v2 on v1

--- a/solution.py
+++ b/solution.py
@@ -142,9 +142,10 @@
 def kernel(
     nx,
     ny,
-    h_ref,
+    h_hbm,
+    k_hbm,
+    out_ref,
     k_ref,
-    out_ref,
     m_ref,
     mt_ref,
     rx_ref,
@@ -171,6 +172,7 @@
     firstx,
     lasty,
     firsty,
+    in_sem,
     hs_sem,
     hr_sem,
     csx,
@@ -184,11 +186,23 @@
 ):
     ix = lax.axis_index("px")
     iy = lax.axis_index("py")
-    planes, rows, columns = h_ref.shape
+    planes, rows, columns = h_hbm.shape
     tiles = columns // LANES
     lx = rows // BLOCKS
     ly = columns // BLOCKS
     turns = (turn0, turn1, turn2)
+
+    def stage(source, target, j, number):
+        return pltpu.make_async_copy(
+            source.at[:, :, pl.ds(j * LANES, LANES)],
+            target.at[pl.ds(j * planes, planes)],
+            in_sem.at[number],
+        )
+
+    stage_k = [stage(k_hbm, k_ref, j, j) for j in range(tiles)]
+    stage_h = [stage(h_hbm, mid_ref, j, tiles + j) for j in range(tiles)]
+    for copy in stage_h:
+        copy.start()
 
     barrier = pltpu.get_barrier_semaphore()
     for d in range(1, nx):
@@ -199,6 +213,9 @@
         pl.semaphore_signal(
             barrier, inc=1, device_id=(ix, lax.rem(iy + d, ny)), device_id_type=MESH
         )
+
+    for copy in stage_k:
+        copy.start()
 
     def peers_x(ref, send, recv):
         return [
@@ -226,22 +243,6 @@
             for d in range(1, ny)
         ]
 
-    for j in range(tiles):
-        at = pl.ds(j * LANES, LANES)
-        part = pl.ds(j * planes, planes)
-        hxs_ref[0, part] = h_ref[:, 0, at]
-        hxs_ref[1, part] = h_ref[:, rows - 1, at]
-    lane = lax.broadcasted_iota(jnp.int32, (rows, LANES), 1)
-    packed = jnp.zeros((rows, LANES), jnp.float32)
-    for p in range(planes):
-        low = h_ref[p, :, 0:LANES]
-        high = h_ref[p, :, columns - LANES : columns]
-        packed = jnp.where(lane == p, low if p == 0 else pltpu.roll(low, p, 1), packed)
-        packed = jnp.where(lane == planes + p, pltpu.roll(high, planes + p + 1, 1), packed)
-    edge = packed.T
-    hys_ref[0] = edge[0:planes]
-    hys_ref[1] = edge[planes : 2 * planes]
-
     @pl.when(ix == 0)
     def _():
         hxr_ref[1] = jnp.zeros_like(hxr_ref[1])
@@ -279,13 +280,29 @@
         (y_up, iy < ny - 1, iy > 0),
     )
 
+    for copy in stage_h:
+        copy.wait()
+    hxs_ref[0] = mid_ref[:, 0, :]
+    hxs_ref[1] = mid_ref[:, rows - 1, :]
+    lane = lax.broadcasted_iota(jnp.int32, (rows, LANES), 1)
+    packed = jnp.zeros((rows, LANES), jnp.float32)
+    for p in range(planes):
+        low = mid_ref[p]
+        high = mid_ref[(tiles - 1) * planes + p]
+        packed = jnp.where(lane == p, low if p == 0 else pltpu.roll(low, p, 1), packed)
+        packed = jnp.where(lane == planes + p, pltpu.roll(high, planes + p + 1, 1), packed)
+    edge = packed.T
+    hys_ref[0] = edge[0:planes]
+    hys_ref[1] = edge[planes : 2 * planes]
+
     pl.semaphore_wait(barrier, nx + ny - 2)
     for copy, sends, _ in routes:
         pl.when(sends)(copy.start)
 
     for j in range(tiles):
-        mid_ref[pl.ds(j * planes, planes)] = h_ref[:, :, pl.ds(j * LANES, LANES)]
-        m_ref[pl.ds(j * planes, planes)] = 1.0 / k_ref[:, :, pl.ds(j * LANES, LANES)]
+        part = pl.ds(j * planes, planes)
+        stage_k[j].wait()
+        m_ref[part] = 1.0 / k_ref[part]
     joined, nodes_x = sweep_coefficients(m_ref, rx_ref, ex_ref, turns, lx)
     for c in range(3):
         cgx[ix, c] = joined[c]
@@ -301,6 +318,7 @@
     send_cy = peers_y(cgy, csy, cry)
     for copy in send_cy:
         copy.start()
+    started = send_cx + send_cy
 
     for copy, _, receives in routes:
         pl.when(receives)(copy.wait_recv)
@@ -369,11 +387,12 @@
         send = peers_x(rgx, rsx, rrx)
         for copy in send:
             copy.start()
+        started.extend(send)
         for copy in send_cx:
-            copy.wait()
+            copy.wait_recv()
         chain = chain_coefficients(cgx, nx)
         for copy in send:
-            copy.wait()
+            copy.wait_recv()
         chain_solve(chain, rgx, lastx, firstx, nx)
         return lastx[ix], firstx[ix]
 
@@ -383,11 +402,12 @@
         send = peers_y(rgy, rsy, rry)
         for copy in send:
             copy.start()
+        started.extend(send)
         for copy in send_cy:
-            copy.wait()
+            copy.wait_recv()
         chain = chain_coefficients(cgy, ny)
         for copy in send:
-            copy.wait()
+            copy.wait_recv()
         chain_solve(chain, rgy, lasty, firsty, ny)
         return lasty[iy], firsty[iy]
 
@@ -418,6 +438,8 @@
             out_ref[p, :, at] = midt_ref[p, at, :].T
     for copy, sends, _ in routes:
         pl.when(sends)(copy.wait_send)
+    for copy in started:
+        copy.wait_send()
 
 
 def on_device(nx, ny, initial_heat_state, spreading_coefficient):
@@ -435,9 +457,10 @@
     return pl.pallas_call(
         functools.partial(kernel, nx, ny),
         out_shape=jax.ShapeDtypeStruct((planes, rows, columns), jnp.float32),
-        in_specs=[pl.BlockSpec(memory_space=pltpu.VMEM)] * 2,
+        in_specs=[pl.BlockSpec(memory_space=pltpu.HBM)] * 2,
         out_specs=pl.BlockSpec(memory_space=pltpu.VMEM),
         scratch_shapes=[
+            vmem(count, rows, LANES),
             vmem(count, rows, LANES),
             vmem(planes, columns, LANES),
             vmem(lx, count, BLOCKS, LANES),
@@ -464,6 +487,7 @@
             vmem(nx, count, LANES),
             vmem(ny, planes, LANES),
             vmem(ny, planes, LANES),
+            dma(2 * (columns // LANES)),
             dma(4),
             dma(4),
             dma(nx - 1),
@@ -478,7 +502,10 @@
         compiler_params=pltpu.CompilerParams(
             collective_id=0, has_side_effects=True, vmem_limit_bytes=32 << 20
         ),
-    )(initial_heat_state, spreading_coefficient)
+    )(
+        pltpu.with_memory_space_constraint(initial_heat_state, pltpu.HBM),
+        pltpu.with_memory_space_constraint(spreading_coefficient, pltpu.HBM),
+    )
 
 
 def solution(mesh):

time: 20.3 us -> 18.3 us (0.901)
  local copies, waits for them, and re-layouts: 2.88 us -> 0.8 us
    unnamed x5 -> x1, local copies, waits for them, and re-layouts: 2.88 us -> 0.8 us
where the time goes in v2:
time: 18.3 us; the launch traced here: 18.1 us
  Pallas kernels  17.3 us (95%)
  local copies, waits for them, and re-layouts  0.8 us (4%)
    pallas_call x1, Pallas kernels, on_device(): pl.pallas_call(functools.partial(kernel, nx, ny), out_shape=jax.ShapeDtyp...  17.3 us
    unnamed x1, local copies, waits for them, and re-layouts  0.8 us

profile of v2, /device:TPU:0, one launch (start us, length us, event | category | flops | bytes accessed | tf_op | source)
XLA Modules:
  0.0 18.1 jit_solution(8516351180582363733)
XLA Ops:
  0.0 17.3 %shard_map.28 = f32[4,128,256]{2,1,0:T(8,128)S(1)} custom-call(f32[4,128,256]{2,1,0:T(8,128)} %h_hbm.1, f32[4,128,256]{2,1,0:T(8,128)} %k_hbm.1), custom_call_target="tpu_custom_call" | custom-call | tf_op jit(solution)/shard_map/pallas_call | solution.py:457
  17.3 0.8 %copy.4 = f32[4,128,256]{2,1,0:T(8,128)} copy(f32[4,128,256]{2,1,0:T(8,128)S(1)} %shard_map.28) | data formatting | bytes 1048576
